TPU v7x, 32 devices: a whole 2x2x4 slice. The times are simulated.
32 devices in a mesh: seq: 16 (over z, y, x), head: 2 (over core).
Axes of the slice: x: 2, y: 2, z: 4, core: 2. Of those that a mesh axis runs over, the one named last changes fastest.
Arguments:
- tokens: bfloat16 [2, 4096, 2048], P(None, 'seq'), may hold values from -6 to 6
- grad_out: bfloat16 [2, 4096, 2048], P(None, 'seq'), may hold values from -6 to 6
- query_weight: bfloat16 [2048, 2048], P('seq', 'head'), may hold values from -0.5 to 0.5
- key_weight: bfloat16 [2048, 2048], P('seq', 'head'), may hold values from -0.5 to 0.5
- value_weight: bfloat16 [2048, 2048], P('seq', 'head'), may hold values from -0.125 to 0.125
- forget_weight: bfloat16 [2048, 256], P('seq', 'head'), may hold values from -0.125 to 0.125
- forget_bias: bfloat16 [4, 64], P('head', 'seq'), as said below
- outgate_weight: bfloat16 [2048, 2048], P('seq', 'head'), may hold values from -0.125 to 0.125
- output_weight: bfloat16 [2048, 2048], P('head', 'seq'), may hold values from -0.125 to 0.125
- slot_gain: bfloat16 [512], P('seq'), may hold values from 0.5 to 1.5
- first_gain: bfloat16 [2048], P('seq'), may hold values from 0.5 to 1.5
- second_gain: bfloat16 [2048], P('seq'), may hold values from 0.5 to 1.5
- gate_weight: bfloat16 [2048, 5632], P('seq', 'head'), may hold values from -0.125 to 0.125
- up_weight: bfloat16 [2048, 5632], P('seq', 'head'), may hold values from -0.125 to 0.125
- down_weight: bfloat16 [5632, 2048], P('head', 'seq'), may hold values from -0.078125 to 0.078125
Outputs:
- output: bfloat16 [2, 4096, 2048], P(None, 'seq')
- input_grad: float32 [2, 4096, 2048], P(None, 'seq')
- query_grad: float32 [2048, 2048], P('seq', 'head')
- key_grad: float32 [2048, 2048], P('seq', 'head')
- value_grad: float32 [2048, 2048], P('seq', 'head')
- forget_grad: float32 [2048, 256], P('seq', 'head')
- forget_bias_grad: float32 [4, 64], P('head', 'seq')
- outgate_grad: float32 [2048, 2048], P('seq', 'head')
- output_grad: float32 [2048, 2048], P('head', 'seq')
- slot_gain_grad: float32 [512], P('seq')
- first_gain_grad: float32 [2048], P('seq')
- second_gain_grad: float32 [2048], P('seq')
- gate_grad: float32 [2048, 5632], P('seq', 'head')
- up_grad: float32 [2048, 5632], P('seq', 'head')
- down_grad: float32 [5632, 2048], P('head', 'seq')
Inputs may be any that keep to these rules, and one draw needn't show every extreme that they name: `forget_bias`: forget gate offsets of the heads and slots, those of per-token decay rates between 0.25 / 4096 and 1 / 30, so about 1 to 9.
All inputs are finite; a program needn't handle non-finite values.
Results may differ from a plain program's by a relative error of at most 0.01655.
Values may be sent and summed in bfloat16 or wider, within the bound.
A program may use at most 320 MiB of HBM per device.

v0:
```python
import jax
import jax.numpy as jnp
from jax import lax
from jax.sharding import PartitionSpec as P

HIGH = lax.Precision.HIGHEST
TAU = 8.0
EPS = 1e-06


def prefix_2(shard, axis, combine, identity):
    size, here = (lax.axis_size(axis), lax.axis_index(axis))
    everything = jax.tree.map(lambda part: lax.all_gather(part, axis), shard)
    start = jax.tree.map(
        lambda part, zero: jnp.broadcast_to(jnp.asarray(zero, part.dtype), part.shape),
        shard,
        identity,
    )

    def prefix_hop(k, before):
        reached = k < here
        new = combine(before, jax.tree.map(lambda part: part[k], everything))
        return jax.tree.map(lambda a, b: jnp.where(reached, a, b), new, before)

    return lax.fori_loop(0, size, prefix_hop, start)


def entering(shard, axis, combine, identity):
    size, here = (lax.axis_size(axis), lax.axis_index(axis))
    everything = jax.tree.map(
        lambda part, kind: lax.all_gather(part.astype(kind), axis),
        shard,
        jax.tree.map(lambda a: jnp.bfloat16 if a.dtype == jnp.float32 else a.dtype, shard),
    )
    start = jax.tree.map(
        lambda part, zero: jnp.broadcast_to(jnp.asarray(zero, part.dtype), part.shape),
        shard,
        identity,
    )

    def entering_hop(k, before):
        at = size - 1 - k
        reached = at > here
        new = combine(
            before, jax.tree.map(lambda part, own: part[at].astype(own.dtype), everything, shard)
        )
        return jax.tree.map(lambda a, b: jnp.where(reached, a, b), new, before)

    return lax.fori_loop(0, size, entering_hop, start)


def rms_scale(values, gain):
    return values * lax.rsqrt(jnp.mean(values * values, axis=-1, keepdims=True) + EPS) * gain


def out_gate(attended, gate, gain):
    return rms_scale(attended, gain) * jax.nn.silu(gate)


def swiglu(ff_gate, ff_up):
    return jax.nn.silu(ff_gate) * ff_up


def silu_slope(values):
    sig = jax.nn.sigmoid(values)
    return sig + values * sig * (1.0 - sig)


def slot_single(query, keys, values, log_decay, keys_in, values_in):
    count = query.shape[0]
    keep = -jnp.expm1(log_decay)
    total = jnp.cumsum(log_decay, axis=0)
    causal = (jnp.arange(count)[:, None] >= jnp.arange(count)[None, :])[:, :, None]
    spread = jnp.where(causal, total[:, None, :] - total[None, :, :], 0.0)
    mixing = jnp.where(causal, jnp.exp(spread), 0.0) * keep[None, :, :]
    scaled = query * query.shape[1] ** (-0.5)
    paired = jnp.dot(scaled, keys.T, precision=HIGH)
    growth = jnp.exp(total)
    scores = jnp.einsum("ts,tsi->ti", paired, mixing, precision=HIGH) + growth * jnp.dot(
        scaled, keys_in.T, precision=HIGH
    )
    probs = jax.nn.softmax(scores, axis=-1)
    weights = jnp.einsum("ti,tsi->ts", probs, mixing, precision=HIGH)
    return jnp.dot(weights, values, precision=HIGH) + jnp.dot(
        probs * growth, values_in, precision=HIGH
    )


def slot_end(keys, values, log_decay):
    total = jnp.cumsum(log_decay, axis=0)
    last = total[-1]
    weight = jnp.exp(last[None, :] - total) * -jnp.expm1(log_decay)
    return (
        jnp.exp(last),
        jnp.dot(weight.T, keys, precision=HIGH),
        jnp.dot(weight.T, values, precision=HIGH),
    )


def heads_attend(query, keys, values, log_decay, keys_in, values_in):

    def one_head(parts):
        return jax.vmap(slot_single)(parts[0], parts[1], parts[2], parts[3], parts[4], parts[5])

    stacked = (
        jnp.moveaxis(query, 2, 0),
        jnp.moveaxis(keys, 2, 0),
        jnp.moveaxis(values, 2, 0),
        jnp.moveaxis(log_decay, 2, 0),
        jnp.moveaxis(keys_in, 1, 0),
        jnp.moveaxis(values_in, 1, 0),
    )
    return jnp.moveaxis(lax.map(jax.checkpoint(one_head), stacked), 0, 2)


def heads_end(keys, values, log_decay):
    inner = jax.vmap(slot_end, in_axes=(1, 1, 1), out_axes=0)
    return jax.vmap(inner, in_axes=(0, 0, 0), out_axes=0)(keys, values, log_decay)


def carry_combine(earlier, later):
    return (
        earlier[0] * later[0],
        later[1] + later[0][..., None] * earlier[1],
        later[2] + later[0][..., None] * earlier[2],
    )


def matmul(left, right):
    return jnp.dot(left, right, preferred_element_type=jnp.float32)


def outer_sum(left, right):
    return jnp.einsum("bti,btj->ij", left, right, preferred_element_type=jnp.float32)


def back_product(grad, weight):
    return jnp.einsum("btj,ij->bti", grad, weight, preferred_element_type=jnp.float32)


def shards(
    tokens,
    grad_out,
    query_weight,
    key_weight,
    value_weight,
    forget_weight,
    forget_bias,
    outgate_weight,
    output_weight,
    slot_gain,
    first_gain,
    second_gain,
    gate_weight,
    up_weight,
    down_weight,
):
    full = (
        lax.all_gather(query_weight, "seq", axis=0, tiled=True),
        lax.all_gather(key_weight, "seq", axis=0, tiled=True),
        lax.all_gather(value_weight, "seq", axis=0, tiled=True),
        lax.all_gather(forget_weight, "seq", axis=0, tiled=True),
        lax.all_gather(forget_bias, "seq", axis=1, tiled=True),
        lax.all_gather(outgate_weight, "seq", axis=0, tiled=True),
        lax.all_gather(output_weight, "seq", axis=1, tiled=True),
        lax.all_gather(slot_gain, "seq", axis=0, tiled=True),
        lax.all_gather(first_gain, "seq", axis=0, tiled=True),
        lax.all_gather(second_gain, "seq", axis=0, tiled=True),
        lax.all_gather(gate_weight, "seq", axis=0, tiled=True),
        lax.all_gather(up_weight, "seq", axis=0, tiled=True),
        lax.all_gather(down_weight, "seq", axis=1, tiled=True),
    )
    query_full = full[0]
    key_full = full[1]
    value_full = full[2]
    forget_full = full[3]
    bias_full = full[4]
    outgate_full = full[5]
    output_full = full[6]
    slot_full = full[7]
    first_full = full[8]
    second_full = full[9]
    gate_full = full[10]
    up_full = full[11]
    down_full = full[12]
    seqs = tokens.shape[0]
    rows = tokens.shape[1]
    heads_here = bias_full.shape[0]
    slots = bias_full.shape[1]
    head_dim = slot_full.shape[0]

    def split_heads(array, inner):
        return array.reshape(seqs, rows, heads_here, inner)

    def join_heads(array):
        return array.reshape(seqs, rows, heads_here * array.shape[3])

    inputs = tokens.astype(jnp.float32)
    normed_one, first_back = jax.vjp(rms_scale, inputs, first_full.astype(jnp.float32))
    normed_one_low = normed_one.astype(jnp.bfloat16)
    query_low = matmul(normed_one_low, query_full).astype(jnp.bfloat16)
    key_low = matmul(normed_one_low, key_full).astype(jnp.bfloat16)
    value_low = matmul(normed_one_low, value_full).astype(jnp.bfloat16)
    forget_logit = matmul(normed_one_low, forget_full) + bias_full.astype(jnp.float32).reshape(
        heads_here * slots
    )
    outgate_pre = matmul(normed_one_low, outgate_full)
    log_decay = split_heads(-jax.nn.softplus(-forget_logit) / TAU, slots)
    query_wide = split_heads(query_low.astype(jnp.float32), head_dim)
    key_wide = split_heads(key_low.astype(jnp.float32), head_dim)
    value_wide = split_heads(value_low.astype(jnp.float32), head_dim)
    query_feat = jax.nn.silu(query_wide)
    key_feat = jax.nn.silu(key_wide)
    decay, local_keys, local_values = heads_end(key_feat, value_wide, log_decay)
    prefix = prefix_2(
        (decay, local_keys, local_values),
        "seq",
        carry_combine,
        (jnp.ones_like(decay), jnp.zeros_like(local_keys), jnp.zeros_like(local_values)),
    )
    keys_in = prefix[1]
    values_in = prefix[2]
    attended, attend_back = jax.vjp(
        heads_attend, query_feat, key_feat, value_wide, log_decay, keys_in, values_in
    )
    gated, gate_back = jax.vjp(
        out_gate, attended, split_heads(outgate_pre, head_dim), slot_full.astype(jnp.float32)
    )
    gated_low = join_heads(gated).astype(jnp.bfloat16)
    mixed = lax.psum(matmul(gated_low, output_full), "head")
    residual = inputs + mixed
    normed_two, second_back = jax.vjp(rms_scale, residual, second_full.astype(jnp.float32))
    normed_two_low = normed_two.astype(jnp.bfloat16)
    ff_gate = matmul(normed_two_low, gate_full)
    ff_up = matmul(normed_two_low, up_full)
    activated_wide, swiglu_back = jax.vjp(swiglu, ff_gate, ff_up)
    activated = activated_wide.astype(jnp.bfloat16)
    ff_out = lax.psum(matmul(activated, down_full).astype(jnp.bfloat16), "head").astype(jnp.float32)
    output = (residual + ff_out).astype(jnp.bfloat16)
    again = (
        lax.all_gather(query_weight, "seq", axis=0, tiled=True),
        lax.all_gather(key_weight, "seq", axis=0, tiled=True),
        lax.all_gather(value_weight, "seq", axis=0, tiled=True),
        lax.all_gather(forget_weight, "seq", axis=0, tiled=True),
        lax.all_gather(forget_bias, "seq", axis=1, tiled=True),
        lax.all_gather(outgate_weight, "seq", axis=0, tiled=True),
        lax.all_gather(output_weight, "seq", axis=1, tiled=True),
        lax.all_gather(slot_gain, "seq", axis=0, tiled=True),
        lax.all_gather(first_gain, "seq", axis=0, tiled=True),
        lax.all_gather(second_gain, "seq", axis=0, tiled=True),
        lax.all_gather(gate_weight, "seq", axis=0, tiled=True),
        lax.all_gather(up_weight, "seq", axis=0, tiled=True),
        lax.all_gather(down_weight, "seq", axis=1, tiled=True),
    )
    query_back = again[0]
    key_back = again[1]
    value_back = again[2]
    forget_back = again[3]
    outgate_back = again[5]
    output_back = again[6]
    gate_back_weight = again[10]
    up_back = again[11]
    down_back = again[12]
    down_grad = outer_sum(activated, grad_out)
    act_grad = back_product(grad_out, down_back)
    gate_wide, up_wide = swiglu_back(act_grad)
    gate_term = gate_wide.astype(jnp.bfloat16)
    up_term = up_wide.astype(jnp.bfloat16)
    gate_grad = outer_sum(normed_two_low, gate_term)
    up_grad = outer_sum(normed_two_low, up_term)
    normed_two_grad = back_product(gate_term, gate_back_weight) + back_product(up_term, up_back)
    normed_two_grad = lax.psum(normed_two_grad.astype(jnp.bfloat16), "head").astype(jnp.float32)
    residual_from_norm, second_gain_grad = second_back(normed_two_grad)
    residual_grad = grad_out.astype(jnp.float32) + residual_from_norm
    residual_low = residual_grad.astype(jnp.bfloat16)
    output_grad = outer_sum(gated_low, residual_low)
    gated_grad = split_heads(back_product(residual_low, output_back), head_dim)
    attended_grad, outgate_wide, slot_gain_grad = gate_back(gated_grad)
    outgate_term = join_heads(outgate_wide).astype(jnp.bfloat16)
    query_part, key_part, value_part, decay_part, keys_in_grad, values_in_grad = attend_back(
        attended_grad
    )
    suffix = entering(
        (decay, keys_in_grad, values_in_grad),
        "seq",
        carry_combine,
        (jnp.ones_like(decay), jnp.zeros_like(keys_in_grad), jnp.zeros_like(values_in_grad)),
    )
    decay_cot = jnp.sum(suffix[1] * keys_in + suffix[2] * values_in, axis=-1)
    ends, end_back = jax.vjp(heads_end, key_feat, value_wide, log_decay)
    key_extra, value_extra, decay_extra = end_back((decay_cot, suffix[1], suffix[2]))
    query_term = join_heads(query_part * silu_slope(query_wide)).astype(jnp.bfloat16)
    key_term = join_heads((key_part + key_extra) * silu_slope(key_wide)).astype(jnp.bfloat16)
    value_term = join_heads(value_part + value_extra).astype(jnp.bfloat16)
    forget_term = (
        join_heads(decay_part + decay_extra) * jax.nn.sigmoid(-forget_logit) / TAU
    ).astype(jnp.bfloat16)
    bias_grad = jnp.sum(forget_term.astype(jnp.float32), axis=(0, 1)).reshape(heads_here, slots)
    query_grad = outer_sum(normed_one_low, query_term)
    key_grad = outer_sum(normed_one_low, key_term)
    value_grad = outer_sum(normed_one_low, value_term)
    forget_grad = outer_sum(normed_one_low, forget_term)
    outgate_grad = outer_sum(normed_one_low, outgate_term)
    normed_one_grad = (
        back_product(query_term, query_back)
        + back_product(key_term, key_back)
        + back_product(value_term, value_back)
        + back_product(forget_term, forget_back)
        + back_product(outgate_term, outgate_back)
    )
    normed_one_grad, slot_gain_grad = (
        lax.psum(normed_one_grad.astype(jnp.bfloat16), "head").astype(jnp.float32),
        lax.psum(slot_gain_grad.astype(jnp.bfloat16), "head").astype(jnp.float32),
    )
    input_from_norm, first_gain_grad = first_back(normed_one_grad)
    input_grad = residual_grad + input_from_norm
    summed = (
        lax.psum_scatter(query_grad, "seq", scatter_dimension=0, tiled=True),
        lax.psum_scatter(key_grad, "seq", scatter_dimension=0, tiled=True),
        lax.psum_scatter(value_grad, "seq", scatter_dimension=0, tiled=True),
        lax.psum_scatter(forget_grad, "seq", scatter_dimension=0, tiled=True),
        lax.psum_scatter(bias_grad, "seq", scatter_dimension=1, tiled=True),
        lax.psum_scatter(outgate_grad, "seq", scatter_dimension=0, tiled=True),
        lax.psum_scatter(output_grad, "seq", scatter_dimension=1, tiled=True),
        lax.psum_scatter(slot_gain_grad, "seq", scatter_dimension=0, tiled=True),
        lax.psum_scatter(first_gain_grad, "seq", scatter_dimension=0, tiled=True),
        lax.psum_scatter(second_gain_grad, "seq", scatter_dimension=0, tiled=True),
        lax.psum_scatter(gate_grad, "seq", scatter_dimension=0, tiled=True),
        lax.psum_scatter(up_grad, "seq", scatter_dimension=0, tiled=True),
        lax.psum_scatter(down_grad, "seq", scatter_dimension=1, tiled=True),
    )
    return (
        output,
        input_grad,
        summed[0],
        summed[1],
        summed[2],
        summed[3],
        summed[4],
        summed[5],
        summed[6],
        summed[7],
        summed[8],
        summed[9],
        summed[10],
        summed[11],
        summed[12],
    )


def solution(mesh):
    return jax.shard_map(
        shards,
        mesh=mesh,
        in_specs=(
            P(None, "seq", None),
            P(None, "seq", None),
            P("seq", "head"),
            P("seq", "head"),
            P("seq", "head"),
            P("seq", "head"),
            P("head", "seq"),
            P("seq", "head"),
            P("head", "seq"),
            P("seq"),
            P("seq"),
            P("seq"),
            P("seq", "head"),
            P("seq", "head"),
            P("head", "seq"),
        ),
        out_specs=(
            P(None, "seq", None),
            P(None, "seq", None),
            P("seq", "head"),
            P("seq", "head"),
            P("seq", "head"),
            P("seq", "head"),
            P("head", "seq"),
            P("seq", "head"),
            P("head", "seq"),
            P("seq"),
            P("seq"),
            P("seq"),
            P("seq", "head"),
            P("seq", "head"),
            P("head", "seq"),
        ),
        check_vma=False,
    )
```

profile of v0, /device:TPU:10, one launch (start us, length us, event | category | flops | bytes accessed | tf_op | source)
XLA Modules:
  0.0 4301.3 jit_solution(4325084734223197280)
XLA Ops:
  40.3 40.7 all-gather.7
  83.5 39.9 all_gather.83
  212.1 39.2 all-gather.1
  274.4 85.9 %all-gather.38.cloned.1.call-done = f32[32,2,64,512]{3,2,1,0:T(8,128)} async-done(((f32[2,2,64,512]{3,2,1,0:T(8,128)}), f32[32,2,64,512]{3,2,1,0:T(8,128)}) %all-gather.38.cloned.1.call-update) | async-done | bytes 8388624 | tf_op jit(solution)/shard_map/all_gather | solution.py:13
  360.3 114.2 %all-gather.40.cloned.1.call-done = f32[32,2,64,512]{3,2,1,0:T(8,128)} async-done(((f32[2,2,64,512]{3,2,1,0:T(8,128)}), f32[32,2,64,512]{3,2,1,0:T(8,128)}) %all-gather.40.cloned.1.call-update) | async-done | bytes 8388624 | tf_op jit(solution)/shard_map/all_gather | solution.py:13
  501.5 167.9 %while.73 = (s32[]{:T(128)}, f32[2,2,256,512]{2,3,0,1:T(8,128)}, f32[2,2,256,512]{3,2,1,0:T(8,128)S(1)}, f32[2,2,256,512]{3,2,1,0:T(8,128)}, f32[2,2,256,64]{2,3...) while((s32[]{:T(128)}, f32[2,2,256,512]{2,3,0,1:T(8,128)}, ...), condition=%wide.region_10.11_spmd.clone.clone, body=%wide.region_5.10_spmd.clone.clone.sunk | while | flops 2287010304 | bytes 27807444 | solution.py:113
  720.5 103.7 %all-gather.36.cloned.1.call-done = bf16[2816,2048]{1,0:T(8,128)(2,1)} async-done(((bf16[2816,128]{1,0:T(8,128)(2,1)}), bf16[2816,2048]{1,0:T(8,128)(2,1)}) %all-gather.36.cloned.1.call-update) | async-done | bytes 11534352 | tf_op jit(solution)/shard_map/all_gather | solution.py:171
  864.4 136.7 %all-gather.34.cloned.1.call-done = bf16[2048,2816]{1,0:T(8,128)(2,1)} async-done(((bf16[128,2816]{1,0:T(8,128)(2,1)}), bf16[2048,2816]{1,0:T(8,128)(2,1)}) %all-gather.34.cloned.1.call-update) | async-done | bytes 11534352 | tf_op jit(solution)/shard_map/all_gather | solution.py:170
  1013.6 131.0 %all-gather.32.cloned.1.call-done = bf16[2048,2816]{1,0:T(8,128)(2,1)} async-done(((bf16[128,2816]{1,0:T(8,128)(2,1)}), bf16[2048,2816]{1,0:T(8,128)(2,1)}) %all-gather.32.cloned.1.call-update) | async-done | bytes 11534352 | tf_op jit(solution)/shard_map/all_gather | solution.py:169
  1228.7 367.7 %while.72 = (s32[]{:T(128)}, f32[2,2,256,512]{2,3,0,1:T(8,128)}, f32[2,2,256,512]{2,3,0,1:T(8,128)}, f32[2,2,256,512]{2,3,0,1:T(8,128)}, f32[2,2,256,64]{2,3,1,0...) while((s32[]{:T(128)}, f32[2,2,256,512]{2,3,0,1:T(8,128)}, ...), condition=%wide.region_29.30_spmd, body=%wide.region_18.29_spmd.sunk | while | flops 5497390080 | bytes 115728032 | solution.py:113
  1249.1 34.8 fusion.380
  1287.6 35.2 fusion.376
  1429.6 34.8 fusion.380
  1468.1 35.4 fusion.376
  1678.0 72.6 %all-gather.44.cloned.1.call-done = bf16[32,2,64,512]{3,2,0,1:T(8,128)(2,1)} async-done(((bf16[2,2,64,512]{3,2,0,1:T(8,128)(2,1)}), bf16[32,2,64,512]{3,2,0,1:T(8,128)(2,1)}) %all-gather.44.cloned.1.call-update) | async-done | bytes 4194320 | tf_op jit(solution)/shard_map/all_gather | solution.py:31
  1912.2 71.2 %all-reduce.6 = (f32[2,64]{1,0:T(2,128)S(1)}, f32[512]{0:T(512)S(1)}, f32[2048]{0:T(1024)S(1)}, f32[2048]{0:T(1024)S(1)}) all-reduce(f32[2,64]{1,0:T(2,128)S(1)} %reshape.331, bf16[512]{0:T(512)(128)(2,1)S(1)} %psum.39, f32[2048]{0:T(1024)S(1)} %get-tuple-element.1070, ...), channel_id=12, replica_groups=mesh['seq'=16,'head'=2] {'seq'}, use_global_device_ids=true, to_apply=%region_43.44.clone | all-reduce | flops 4736 | bytes 36864
  1993.1 121.7 %reduce-scatter.21.cloned.1.call-done = f32[1024,128]{1,0:T(8,128)} async-done(((f32[1024,2048]{1,0:T(8,128)}), f32[1024,128]{1,0:T(8,128)}) %reduce-scatter.21.cloned.1.call-update) | async-done | bytes 524304 | tf_op jit(solution)/shard_map/reduce_scatter | solution.py:324
  2114.8 183.0 %reduce-scatter.11.cloned.1.call-done = f32[128,1024]{1,0:T(8,128)} async-done(((f32[2048,1024]{1,0:T(8,128)}), f32[128,1024]{1,0:T(8,128)}) %reduce-scatter.11.cloned.1.call-update) | async-done | bytes 524304 | tf_op jit(solution)/shard_map/reduce_scatter | solution.py:318
  2297.8 183.1 %reduce-scatter.19.cloned.1.call-done = f32[128,1024]{1,0:T(8,128)} async-done(((f32[2048,1024]{1,0:T(8,128)}), f32[128,1024]{1,0:T(8,128)}) %reduce-scatter.19.cloned.1.call-update) | async-done | bytes 524304 | tf_op jit(solution)/shard_map/reduce_scatter | solution.py:323
  2480.9 183.0 %reduce-scatter.13.cloned.1.call-done = f32[128,1024]{1,0:T(8,128)} async-done(((f32[2048,1024]{1,0:T(8,128)}), f32[128,1024]{1,0:T(8,128)}) %reduce-scatter.13.cloned.1.call-update) | async-done | bytes 524304 | tf_op jit(solution)/shard_map/reduce_scatter | solution.py:319
  2663.9 183.1 %reduce-scatter.15.cloned.1.call-done = f32[128,1024]{1,0:T(8,128)} async-done(((f32[2048,1024]{1,0:T(8,128)}), f32[128,1024]{1,0:T(8,128)}) %reduce-scatter.15.cloned.1.call-update) | async-done | bytes 524304 | tf_op jit(solution)/shard_map/reduce_scatter | solution.py:320
  2847.0 482.0 %reduce-scatter.23.cloned.1.call-done = f32[128,2816]{1,0:T(8,128)} async-done(((f32[2048,2816]{1,0:T(8,128)}), f32[128,2816]{1,0:T(8,128)}) %reduce-scatter.23.cloned.1.call-update) | async-done | bytes 1441808 | tf_op jit(solution)/shard_map/reduce_scatter | solution.py:328
  3329.0 482.7 %reduce-scatter.25.cloned.1.call-done = f32[128,2816]{1,0:T(8,128)} async-done(((f32[2048,2816]{1,0:T(8,128)}), f32[128,2816]{1,0:T(8,128)}) %reduce-scatter.25.cloned.1.call-update) | async-done | bytes 1441808 | tf_op jit(solution)/shard_map/reduce_scatter | solution.py:329
  3811.7 482.5 %reduce-scatter.27.cloned.1.call-done = f32[2816,128]{1,0:T(8,128)} async-done(((f32[2816,2048]{1,0:T(8,128)}), f32[2816,128]{1,0:T(8,128)}) %reduce-scatter.27.cloned.1.call-update) | async-done | bytes 1441808 | tf_op jit(solution)/shard_map/reduce_scatter | solution.py:330
  (580 shorter events, 1024.4 us)
Async XLA Ops:
  7.2 128.0 %all-gather.24.cloned.1.call-start = ((), (), s32[]{:S(2)}) async-start(), calls=%async_computation.10 | async-start | bytes 4456448 | tf_op jit(solution)/shard_map/all_gather | solution.py:160
  7.9 160.8 %all-gather.26.cloned.1.call-start = ((), (), s32[]{:S(2)}) async-start(), calls=%async_computation.11 | async-start | bytes 4456448 | tf_op jit(solution)/shard_map/all_gather | solution.py:161
  8.7 249.8 %all-gather.22.cloned.1.call-start = ((), (), s32[]{:S(2)}) async-start(), calls=%async_computation.9 | async-start | bytes 4456448 | tf_op jit(solution)/shard_map/all_gather | solution.py:159
  9.4 350.9 %all-gather.38.cloned.1.call-start = ((), (), s32[]{:S(2)}) async-start(), calls=%async_computation.28 | async-start | bytes 8912896 | tf_op jit(solution)/shard_map/all_gather | solution.py:13
  148.9 325.7 %all-gather.40.cloned.1.call-start = ((), (), s32[]{:S(2)}) async-start(), calls=%async_computation.29 | async-start | bytes 8912896 | tf_op jit(solution)/shard_map/all_gather | solution.py:13
  175.8 495.4 %all-gather.28.cloned.1.call-start = ((), (), s32[]{:S(2)}) async-start(), calls=%async_computation.12 | async-start | bytes 4456448 | tf_op jit(solution)/shard_map/all_gather | solution.py:164
  176.4 502.7 %all-gather.30.cloned.1.call-start = ((), (), s32[]{:S(2)}) async-start(), calls=%async_computation.13 | async-start | bytes 4456448 | tf_op jit(solution)/shard_map/all_gather | solution.py:165
  177.1 647.1 %all-gather.36.cloned.1.call-start = ((), (), s32[]{:S(2)}) async-start(), calls=%async_computation.17 | async-start | bytes 12255232 | tf_op jit(solution)/shard_map/all_gather | solution.py:171
  177.8 679.2 %all-reduce.12.cloned.1.call-start = ((), (), s32[]{:S(2)}) async-start(), calls=%async_computation.14 | async-start | bytes 8388608 | tf_op jit(solution)/shard_map/psum | solution.py:230
  686.0 315.0 %all-gather.34.cloned.1.call-start = ((), (), s32[]{:S(2)}) async-start(), calls=%async_computation.16 | async-start | bytes 12255232 | tf_op jit(solution)/shard_map/all_gather | solution.py:170
  686.6 458.0 %all-gather.32.cloned.1.call-start = ((), (), s32[]{:S(2)}) async-start(), calls=%async_computation.15 | async-start | bytes 12255232 | tf_op jit(solution)/shard_map/all_gather | solution.py:169
  687.4 517.5 %all-reduce.14.cloned.1.call-start = ((), (), s32[]{:S(2)}) async-start(), calls=%async_computation.18 | async-start | bytes 4194304 | tf_op jit(solution)/shard_map/psum | solution.py:272
  1183.0 490.2 %all-gather.42.cloned.1.call-start = ((), (), s32[]{:S(2)}) async-start(), calls=%async_computation.30 | async-start | bytes 4456448 | tf_op jit(solution)/shard_map/all_gather | solution.py:31
  1596.5 154.1 %all-gather.44.cloned.1.call-start = ((), (), s32[]{:S(2)}) async-start(), calls=%async_computation.31 | async-start | bytes 4456448 | tf_op jit(solution)/shard_map/all_gather | solution.py:31
  1597.1 311.8 %all-reduce.16.cloned.1.call-start = ((), (), s32[]{:S(2)}) async-start(), calls=%async_computation.32 | async-start | bytes 8388608 | tf_op jit(solution)/shard_map/psum | solution.py:238
  1823.9 169.2 %reduce-scatter.17.cloned.1.call-start = ((), (), s32[]{:S(2)}) async-start(), calls=%async_computation.22 | async-start | bytes 1114112 | tf_op jit(solution)/shard_map/reduce_scatter | solution.py:321
  1827.5 287.3 %reduce-scatter.21.cloned.1.call-start = ((), (), s32[]{:S(2)}) async-start(), calls=%async_computation.24 | async-start | bytes 8912896 | tf_op jit(solution)/shard_map/reduce_scatter | solution.py:324
  1835.9 461.9 %reduce-scatter.11.cloned.1.call-start = ((), (), s32[]{:S(2)}) async-start(), calls=%async_computation.19 | async-start | bytes 8912896 | tf_op jit(solution)/shard_map/reduce_scatter | solution.py:318
  1843.0 637.9 %reduce-scatter.19.cloned.1.call-start = ((), (), s32[]{:S(2)}) async-start(), calls=%async_computation.23 | async-start | bytes 8912896 | tf_op jit(solution)/shard_map/reduce_scatter | solution.py:323
  1850.6 813.3 %reduce-scatter.13.cloned.1.call-start = ((), (), s32[]{:S(2)}) async-start(), calls=%async_computation.20 | async-start | bytes 8912896 | tf_op jit(solution)/shard_map/reduce_scatter | solution.py:319
  1857.8 989.2 %reduce-scatter.15.cloned.1.call-start = ((), (), s32[]{:S(2)}) async-start(), calls=%async_computation.21 | async-start | bytes 8912896 | tf_op jit(solution)/shard_map/reduce_scatter | solution.py:320
  1865.0 1464.1 %reduce-scatter.23.cloned.1.call-start = ((), (), s32[]{:S(2)}) async-start(), calls=%async_computation.25 | async-start | bytes 24510464 | tf_op jit(solution)/shard_map/reduce_scatter | solution.py:328
  1878.1 1933.6 %reduce-scatter.25.cloned.1.call-start = ((), (), s32[]{:S(2)}) async-start(), calls=%async_computation.26 | async-start | bytes 24510464 | tf_op jit(solution)/shard_map/reduce_scatter | solution.py:329
  1891.1 2403.1 %reduce-scatter.27.cloned.1.call-start = ((), (), s32[]{:S(2)}) async-start(), calls=%async_computation.27 | async-start | bytes 24510464 | tf_op jit(solution)/shard_map/reduce_scatter | solution.py:330
  (101 other events, 1403.6 us)
Sparse Core Ops, SparseCore 0:
  10.8 76.9 all-gather.23
  90.6 78.1 all-gather.25
  171.5 75.1 all-gather.21
  250.0 110.3 all-gather.37
  363.5 111.0 all-gather.39
  477.2 75.6 all-gather.27
  555.6 85.0 all-gather.29
  643.3 180.8 all-gather.35
  827.3 29.7 all-reduce.11
  860.0 141.0 all-gather.33
  1004.2 140.3 all-gather.31
  1183.1 21.6 all-reduce.13
  1596.6 76.6 all-gather.41
  1675.9 74.6 all-gather.43
  1824.0 27.7 all-reduce.15
  1854.6 67.9 reduce-scatter.16
  1925.3 189.4 reduce-scatter.20
  2117.5 180.1 reduce-scatter.10
  2300.6 180.2 reduce-scatter.18
  2483.6 180.2 reduce-scatter.12
  2666.7 180.2 reduce-scatter.14
  2849.9 479.0 reduce-scatter.22
  3331.9 479.7 reduce-scatter.24
  3814.4 479.7 reduce-scatter.26
where the time goes:
time: 4310 us; the launch traced here: 4300 us
  waiting for transfers between devices  3040 us (71%)
  matrix products  532 us (12%)
  blocking collectives  318 us (7%)
  other arithmetic  246 us (6%)
  local copies, waits for them, and re-layouts  123 us (3%)
    reduce_scatter x1, waiting for transfers between devices, shards(): lax.psum_scatter(up_grad, 'seq', scatter_dimension=0, tiled=True)  483 us
    reduce_scatter x1, waiting for transfers between devices, shards(): lax.psum_scatter(down_grad, 'seq', scatter_dimension=1, tiled=True)  483 us
    reduce_scatter x1, waiting for transfers between devices, shards(): lax.psum_scatter(gate_grad, 'seq', scatter_dimension=0, tiled=True)  482 us
    all_gather x2, waiting for transfers between devices, prefix_2(): everything = jax.tree.map(lambda part: lax.all_gather(part, axis), shard)  200 us
    reduce_scatter x1, waiting for transfers between devices, shards(): lax.psum_scatter(value_grad, 'seq', scatter_dimension=0, tiled=True)  183 us
    reduce_scatter x1, waiting for transfers between devices, shards(): lax.psum_scatter(outgate_grad, 'seq', scatter_dimension=0, tiled=True)  183 us
    reduce_scatter x1, waiting for transfers between devices, shards(): lax.psum_scatter(key_grad, 'seq', scatter_dimension=0, tiled=True)  183 us
    reduce_scatter x1, waiting for transfers between devices, shards(): lax.psum_scatter(query_grad, 'seq', scatter_dimension=0, tiled=True)  183 us
  transfers between devices with their start and end apart: 24, of which 18 were waited for; matrix products, arithmetic and copies ran while one was open for 9% of the time, Pallas kernels for 0%

commit v1 on v0

--- a/solution.py
+++ b/solution.py
@@ -6,6 +6,24 @@
 HIGH = lax.Precision.HIGHEST
 TAU = 8.0
 EPS = 1e-06
+
+
+def collect(value, axis, dim):
+    ways, here, turn = (lax.axis_size(axis), lax.axis_index(axis), value.shape[dim])
+    dims = [n * ways if d == dim else n for d, n in enumerate(value.shape)]
+    full = lax.dynamic_update_slice_in_dim(
+        jnp.zeros(dims, value.dtype), value, here * turn, axis=dim
+    )
+    going_up = going_down = value
+    for far in range(1, ways // 2 + 1):
+        going_up = lax.ppermute(going_up, axis, [(d, (d + 1) % ways) for d in range(ways)])
+        full = lax.dynamic_update_slice_in_dim(full, going_up, (here - far) % ways * turn, axis=dim)
+        if 2 * far < ways:
+            going_down = lax.ppermute(going_down, axis, [(d, (d - 1) % ways) for d in range(ways)])
+            full = lax.dynamic_update_slice_in_dim(
+                full, going_down, (here + far) % ways * turn, axis=dim
+            )
+    return full
 
 
 def prefix_2(shard, axis, combine, identity):
@@ -168,7 +186,7 @@
         lax.all_gather(second_gain, "seq", axis=0, tiled=True),
         lax.all_gather(gate_weight, "seq", axis=0, tiled=True),
         lax.all_gather(up_weight, "seq", axis=0, tiled=True),
-        lax.all_gather(down_weight, "seq", axis=1, tiled=True),
+        collect(down_weight, "seq", 1),
     )
     query_full = full[0]
     key_full = full[1]

time: 4310 us -> 4500 us (1.044)
  waiting for transfers between devices: 3040 us -> 3200 us
    ppermute x0 -> x15, waiting for transfers between devices: none -> 233 us  [the longest x8 180 us: collect(): lax.ppermute(going_up, axis, [(d, (d + 1) % ways) for d in range(ways)])]
    all_gather x2, waiting for transfers between devices: 95.1 us -> 0.01 us  [entering(): lax.all_gather(part.astype(kind), axis)]
    reduce_scatter x1, waiting for transfers between devices: 122 us -> 183 us  [shards(): lax.psum_scatter(output_grad, 'seq', scatter_dimension=1, tiled=True)]
    reduce_scatter x1, waiting for transfers between devices: 183 us -> 122 us  [shards(): lax.psum_scatter(query_grad, 'seq', scatter_dimension=0, tiled=True)]
  transfers between devices with their start and end apart: 24 -> 39, of which waited for: 18 -> 28; matrix products, arithmetic and copies ran while one was open for 9% -> 9% of each run, Pallas kernels for 0% -> 0%
where the time goes in v1:
time: 4500 us; the launch traced here: 4490 us
  waiting for transfers between devices  3200 us (71%)
  matrix products  536 us (12%)
  blocking collectives  334 us (7%)
  other arithmetic  235 us (5%)
  local copies, waits for them, and re-layouts  136 us (3%)
    reduce_scatter x1, waiting for transfers between devices, shards(): lax.psum_scatter(up_grad, 'seq', scatter_dimension=0, tiled=True)  483 us
    reduce_scatter x1, waiting for transfers between devices, shards(): lax.psum_scatter(down_grad, 'seq', scatter_dimension=1, tiled=True)  483 us
    reduce_scatter x1, waiting for transfers between devices, shards(): lax.psum_scatter(gate_grad, 'seq', scatter_dimension=0, tiled=True)  482 us
    all_gather x2, waiting for transfers between devices, prefix_2(): everything = jax.tree.map(lambda part: lax.all_gather(part, axis), shard)  202 us
    reduce_scatter x1, waiting for transfers between devices, shards(): lax.psum_scatter(outgate_grad, 'seq', scatter_dimension=0, tiled=True)  183 us
    reduce_scatter x1, waiting for transfers between devices, shards(): lax.psum_scatter(value_grad, 'seq', scatter_dimension=0, tiled=True)  183 us
    reduce_scatter x1, waiting for transfers between devices, shards(): lax.psum_scatter(output_grad, 'seq', scatter_dimension=1, tiled=True)  183 us
    reduce_scatter x1, waiting for transfers between devices, shards(): lax.psum_scatter(key_grad, 'seq', scatter_dimension=0, tiled=True)  183 us
  transfers between devices with their start and end apart: 39, of which 28 were waited for; matrix products, arithmetic and copies ran while one was open for 9% of the time, Pallas kernels for 0%

profile of v1, /device:TPU:10, one launch (start us, length us, event | category | flops | bytes accessed | tf_op | source)
XLA Modules:
  0.0 4486.1 jit_solution(17276694482927609251)
XLA Ops:
  39.4 40.7 all-gather.7
  83.4 39.9 all_gather.82
  212.1 39.1 all-gather.1
  273.0 87.3 %all-gather.38.cloned.1.call-done = f32[32,2,64,512]{3,2,1,0:T(8,128)} async-done(((f32[2,2,64,512]{3,2,1,0:T(8,128)}), f32[32,2,64,512]{3,2,1,0:T(8,128)}) %all-gather.38.cloned.1.call-update) | async-done | bytes 8388624 | tf_op jit(solution)/shard_map/all_gather | solution.py:31
  360.3 114.2 %all-gather.40.cloned.1.call-done = f32[32,2,64,512]{3,2,1,0:T(8,128)} async-done(((f32[2,2,64,512]{3,2,1,0:T(8,128)}), f32[32,2,64,512]{3,2,1,0:T(8,128)}) %all-gather.40.cloned.1.call-update) | async-done | bytes 8388624 | tf_op jit(solution)/shard_map/all_gather | solution.py:31
  501.6 139.9 %while.73 = (s32[]{:T(128)}, f32[2,2,256,512]{2,3,0,1:T(8,128)}, f32[2,2,256,512]{3,2,1,0:T(8,128)}, f32[2,2,256,512]{3,2,1,0:T(8,128)}, f32[2,2,256,64]{2,3,1,0...) while((s32[]{:T(128)}, f32[2,2,256,512]{2,3,0,1:T(8,128)}, ...), condition=%wide.region_10.11_spmd.clone.clone, body=%wide.region_5.10_spmd.clone.clone.sunk | while | flops 2287010304 | bytes 26756780 | solution.py:131
  694.1 130.1 %all-gather.36.cloned.1.call-done = bf16[2816,2048]{1,0:T(8,128)(2,1)} async-done(((bf16[2816,128]{1,0:T(8,128)(2,1)}), bf16[2816,2048]{1,0:T(8,128)(2,1)}) %all-gather.36.cloned.1.call-update) | async-done | bytes 11534352 | tf_op jit(solution)/shard_map/all_gather | solution.py:271
  862.2 138.8 %all-gather.34.cloned.1.call-done = bf16[2048,2816]{1,0:T(8,128)(2,1)} async-done(((bf16[128,2816]{1,0:T(8,128)(2,1)}), bf16[2048,2816]{1,0:T(8,128)(2,1)}) %all-gather.34.cloned.1.call-update) | async-done | bytes 11534352 | tf_op jit(solution)/shard_map/all_gather | solution.py:188
  1012.1 132.4 %all-gather.32.cloned.1.call-done = bf16[2048,2816]{1,0:T(8,128)(2,1)} async-done(((bf16[128,2816]{1,0:T(8,128)(2,1)}), bf16[2048,2816]{1,0:T(8,128)(2,1)}) %all-gather.32.cloned.1.call-update) | async-done | bytes 11534352 | tf_op jit(solution)/shard_map/all_gather | solution.py:187
  1224.0 363.3 %while.72 = (s32[]{:T(128)}, f32[2,2,256,512]{2,3,0,1:T(8,128)}, f32[2,2,256,512]{2,3,0,1:T(8,128)}, f32[2,2,256,512]{2,3,0,1:T(8,128)}, f32[2,2,256,64]{2,3,1,0...) while((s32[]{:T(128)}, f32[2,2,256,512]{2,3,0,1:T(8,128)}, ...), condition=%wide.region_29.30_spmd, body=%wide.region_18.29_spmd.sunk | while | flops 5497390080 | bytes 98163696 | solution.py:131
  1242.0 35.2 fusion.376
  1465.5 35.2 fusion.380
  1625.4 38.0 collective-permute-done.2
  1672.1 39.7 collective-permute-done.4
  1711.8 38.8 all-gather.5
  2089.9 77.7 %all-reduce.6 = (f32[2,64]{1,0:T(2,128)S(1)}, f32[512]{0:T(512)S(1)}, f32[2048]{0:T(1024)S(1)}, f32[2048]{0:T(1024)S(1)}) all-reduce(f32[2,64]{1,0:T(2,128)S(1)} %reshape.331, bf16[512]{0:T(512)(128)(2,1)S(1)} %psum.39, f32[2048]{0:T(1024)S(1)} %get-tuple-element.1070, ...), channel_id=12, replica_groups=mesh['seq'=16,'head'=2] {'seq'}, use_global_device_ids=true, to_apply=%region_43.44.clone | all-reduce | flops 4736 | bytes 36864
  2177.4 121.7 %reduce-scatter.11.cloned.1.call-done = f32[128,1024]{1,0:T(8,128)} async-done(((f32[2048,1024]{1,0:T(8,128)}), f32[128,1024]{1,0:T(8,128)}) %reduce-scatter.11.cloned.1.call-update) | async-done | bytes 524304 | tf_op jit(solution)/shard_map/reduce_scatter | solution.py:336
  2299.1 183.2 %reduce-scatter.19.cloned.1.call-done = f32[128,1024]{1,0:T(8,128)} async-done(((f32[2048,1024]{1,0:T(8,128)}), f32[128,1024]{1,0:T(8,128)}) %reduce-scatter.19.cloned.1.call-update) | async-done | bytes 524304 | tf_op jit(solution)/shard_map/reduce_scatter | solution.py:341
  2482.3 183.1 %reduce-scatter.21.cloned.1.call-done = f32[1024,128]{1,0:T(8,128)} async-done(((f32[1024,2048]{1,0:T(8,128)}), f32[1024,128]{1,0:T(8,128)}) %reduce-scatter.21.cloned.1.call-update) | async-done | bytes 524304 | tf_op jit(solution)/shard_map/reduce_scatter | solution.py:342
  2665.4 183.0 %reduce-scatter.13.cloned.1.call-done = f32[128,1024]{1,0:T(8,128)} async-done(((f32[2048,1024]{1,0:T(8,128)}), f32[128,1024]{1,0:T(8,128)}) %reduce-scatter.13.cloned.1.call-update) | async-done | bytes 524304 | tf_op jit(solution)/shard_map/reduce_scatter | solution.py:337
  2848.4 183.1 %reduce-scatter.15.cloned.1.call-done = f32[128,1024]{1,0:T(8,128)} async-done(((f32[2048,1024]{1,0:T(8,128)}), f32[128,1024]{1,0:T(8,128)}) %reduce-scatter.15.cloned.1.call-update) | async-done | bytes 524304 | tf_op jit(solution)/shard_map/reduce_scatter | solution.py:338
  3031.6 482.0 %reduce-scatter.23.cloned.1.call-done = f32[128,2816]{1,0:T(8,128)} async-done(((f32[2048,2816]{1,0:T(8,128)}), f32[128,2816]{1,0:T(8,128)}) %reduce-scatter.23.cloned.1.call-update) | async-done | bytes 1441808 | tf_op jit(solution)/shard_map/reduce_scatter | solution.py:346
  3513.6 482.7 %reduce-scatter.25.cloned.1.call-done = f32[128,2816]{1,0:T(8,128)} async-done(((f32[2048,2816]{1,0:T(8,128)}), f32[128,2816]{1,0:T(8,128)}) %reduce-scatter.25.cloned.1.call-update) | async-done | bytes 1441808 | tf_op jit(solution)/shard_map/reduce_scatter | solution.py:347
  3996.3 482.5 %reduce-scatter.27.cloned.1.call-done = f32[2816,128]{1,0:T(8,128)} async-done(((f32[2816,2048]{1,0:T(8,128)}), f32[2816,128]{1,0:T(8,128)}) %reduce-scatter.27.cloned.1.call-update) | async-done | bytes 1441808 | tf_op jit(solution)/shard_map/reduce_scatter | solution.py:348
  (679 shorter events, 1217.7 us)
Async XLA Ops:
  7.2 127.4 %all-gather.24.cloned.1.call-start = ((), (), s32[]{:S(2)}) async-start(), calls=%async_computation.10 | async-start | bytes 4456448 | tf_op jit(solution)/shard_map/all_gather | solution.py:178
  7.9 160.8 %all-gather.26.cloned.1.call-start = ((), (), s32[]{:S(2)}) async-start(), calls=%async_computation.11 | async-start | bytes 4456448 | tf_op jit(solution)/shard_map/all_gather | solution.py:179
  8.7 243.2 %all-gather.22.cloned.1.call-start = ((), (), s32[]{:S(2)}) async-start(), calls=%async_computation.9 | async-start | bytes 4456448 | tf_op jit(solution)/shard_map/all_gather | solution.py:177
  9.4 350.9 %all-gather.38.cloned.1.call-start = ((), (), s32[]{:S(2)}) async-start(), calls=%async_computation.28 | async-start | bytes 8912896 | tf_op jit(solution)/shard_map/all_gather | solution.py:31
  148.5 326.0 %all-gather.40.cloned.1.call-start = ((), (), s32[]{:S(2)}) async-start(), calls=%async_computation.29 | async-start | bytes 8912896 | tf_op jit(solution)/shard_map/all_gather | solution.py:31
  175.8 467.6 %all-gather.28.cloned.1.call-start = ((), (), s32[]{:S(2)}) async-start(), calls=%async_computation.12 | async-start | bytes 4456448 | tf_op jit(solution)/shard_map/all_gather | solution.py:182
  176.4 474.6 %all-gather.30.cloned.1.call-start = ((), (), s32[]{:S(2)}) async-start(), calls=%async_computation.13 | async-start | bytes 4456448 | tf_op jit(solution)/shard_map/all_gather | solution.py:183
  177.1 647.0 %all-gather.36.cloned.1.call-start = ((), (), s32[]{:S(2)}) async-start(), calls=%async_computation.17 | async-start | bytes 12255232 | tf_op jit(solution)/shard_map/all_gather | solution.py:271
  177.9 679.1 %all-reduce.12.cloned.1.call-start = ((), (), s32[]{:S(2)}) async-start(), calls=%async_computation.14 | async-start | bytes 8388608 | tf_op jit(solution)/shard_map/psum | solution.py:248
  658.2 342.8 %all-gather.34.cloned.1.call-start = ((), (), s32[]{:S(2)}) async-start(), calls=%async_computation.16 | async-start | bytes 12255232 | tf_op jit(solution)/shard_map/all_gather | solution.py:188
  658.8 485.7 %all-gather.32.cloned.1.call-start = ((), (), s32[]{:S(2)}) async-start(), calls=%async_computation.15 | async-start | bytes 12255232 | tf_op jit(solution)/shard_map/all_gather | solution.py:187
  659.6 541.6 %all-reduce.14.cloned.1.call-start = ((), (), s32[]{:S(2)}) async-start(), calls=%async_computation.18 | async-start | bytes 4194304 | tf_op jit(solution)/shard_map/psum | solution.py:290
  1179.3 746.3 %all-gather.42.cloned.1.call-start = ((), (), s32[]{:S(2)}) async-start(), calls=%async_computation.30 | async-start | bytes 4456448 | tf_op jit(solution)/shard_map/all_gather | solution.py:49
  1587.4 342.9 %all-gather.44.cloned.1.call-start = ((), (), s32[]{:S(2)}) async-start(), calls=%async_computation.31 | async-start | bytes 4456448 | tf_op jit(solution)/shard_map/all_gather | solution.py:49
  1757.7 328.9 %all-reduce.16.cloned.1.call-start = ((), (), s32[]{:S(2)}) async-start(), calls=%async_computation.32 | async-start | bytes 8388608 | tf_op jit(solution)/shard_map/psum | solution.py:256
  2001.2 176.2 %reduce-scatter.17.cloned.1.call-start = ((), (), s32[]{:S(2)}) async-start(), calls=%async_computation.22 | async-start | bytes 1114112 | tf_op jit(solution)/shard_map/reduce_scatter | solution.py:339
  2004.7 294.4 %reduce-scatter.11.cloned.1.call-start = ((), (), s32[]{:S(2)}) async-start(), calls=%async_computation.19 | async-start | bytes 8912896 | tf_op jit(solution)/shard_map/reduce_scatter | solution.py:336
  2010.7 471.6 %reduce-scatter.19.cloned.1.call-start = ((), (), s32[]{:S(2)}) async-start(), calls=%async_computation.23 | async-start | bytes 8912896 | tf_op jit(solution)/shard_map/reduce_scatter | solution.py:341
  2018.6 646.8 %reduce-scatter.21.cloned.1.call-start = ((), (), s32[]{:S(2)}) async-start(), calls=%async_computation.24 | async-start | bytes 8912896 | tf_op jit(solution)/shard_map/reduce_scatter | solution.py:342
  2027.7 820.7 %reduce-scatter.13.cloned.1.call-start = ((), (), s32[]{:S(2)}) async-start(), calls=%async_computation.20 | async-start | bytes 8912896 | tf_op jit(solution)/shard_map/reduce_scatter | solution.py:337
  2035.2 996.3 %reduce-scatter.15.cloned.1.call-start = ((), (), s32[]{:S(2)}) async-start(), calls=%async_computation.21 | async-start | bytes 8912896 | tf_op jit(solution)/shard_map/reduce_scatter | solution.py:338
  2042.3 1471.3 %reduce-scatter.23.cloned.1.call-start = ((), (), s32[]{:S(2)}) async-start(), calls=%async_computation.25 | async-start | bytes 24510464 | tf_op jit(solution)/shard_map/reduce_scatter | solution.py:346
  2055.7 1940.6 %reduce-scatter.25.cloned.1.call-start = ((), (), s32[]{:S(2)}) async-start(), calls=%async_computation.26 | async-start | bytes 24510464 | tf_op jit(solution)/shard_map/reduce_scatter | solution.py:347
  2068.9 2410.0 %reduce-scatter.27.cloned.1.call-start = ((), (), s32[]{:S(2)}) async-start(), calls=%async_computation.27 | async-start | bytes 24510464 | tf_op jit(solution)/shard_map/reduce_scatter | solution.py:348
  (142 other events, 3375.2 us)
Sparse Core Ops, SparseCore 0:
  10.8 76.9 all-gather.23
  90.6 78.1 all-gather.25
  171.5 75.1 all-gather.21
  250.0 110.3 all-gather.37
  363.5 111.0 all-gather.39
  477.2 75.6 all-gather.27
  555.6 84.9 all-gather.29
  643.3 180.7 all-gather.35
  827.2 29.7 all-reduce.11
  859.9 141.0 all-gather.33
  1004.1 140.3 all-gather.31
  1179.4 21.6 all-reduce.13
  1587.5 136.2 all-gather.41
  1757.8 134.9 all-gather.43
  2001.3 34.8 all-reduce.15
  2039.0 67.9 reduce-scatter.16
  2109.6 189.4 reduce-scatter.10
  2301.8 180.4 reduce-scatter.18
  2485.2 180.2 reduce-scatter.20
  2668.1 180.2 reduce-scatter.12
  2851.3 180.2 reduce-scatter.14
  3034.4 479.1 reduce-scatter.22
  3516.5 479.7 reduce-scatter.24
  3999.0 479.7 reduce-scatter.26
